TPU v7x, 32 devices: a whole 2x2x4 slice. The times are simulated.
32 devices in a mesh: wide: 16 (over z, y, x), narrow: 2 (over core).
Axes of the slice: x: 2, y: 2, z: 4, core: 2. Of those that a mesh axis runs over, the one named last changes fastest.
Arguments:
- grads: bfloat16 [14, 512, 2048], P(None, 'wide', 'narrow'), may hold values from -200 to 200
- momentum: float32 [14, 512, 2048], P(None, 'wide', 'narrow'), may hold values from -400 to 400
- owners: int32 [14], replicated, may hold values from 0 to 15, as said below
- norm_grads: float32 [28, 2048], P('narrow', 'wide'), may hold values from -6 to 6
- norm_params: float32 [28, 2048], P('narrow', 'wide'), may hold values from 0.5 to 1.5
- adam_m: float32 [28, 2048], P('narrow', 'wide'), may hold values from -4 to 4
- adam_v: float32 [28, 2048], P('narrow', 'wide'), may hold values from 0.1 to 4
Outputs:
- muon_update: bfloat16 [14, 512, 2048], P(None, 'wide', 'narrow')
- momentum_new: float32 [14, 512, 2048], P(None, 'wide', 'narrow')
- owner_load: float32 [16], P('wide')
- norm_params_new: float32 [28, 2048], P('narrow', 'wide')
- adam_m_new: float32 [28, 2048], P('narrow', 'wide')
- adam_v_new: float32 [28, 2048], P('narrow', 'wide')
Inputs may be any that keep to these rules, and one draw needn't show every extreme that they name: `owners`: each of the 16 groups owns at most 2 matrices, and some group owns exactly 2.
All inputs are finite; a program needn't handle non-finite values.
Results may differ from a plain program's by a relative error of at most 0.014.
Values may be sent and summed in bfloat16 or wider, within the bound.
A program may use at most 64 MiB of HBM per device.

v0:
```python
import math

import jax
import jax.numpy as jnp
from jax import lax
from jax.sharding import PartitionSpec as P

D = 2048
KV_OUT = 512
ITERS = 2


coef_a = 3.4445
coef_b = -4.775
coef_c = 2.0315
muon_beta = 0.95
norm_eps = 1e-07
adam_first = 0.9
adam_second = 0.95
adam_rate = 0.02
adam_eps = 1e-08
first_fix = 1.0 - 0.9**10
second_fix = 1.0 - 0.95**10


def polynomial_times(current, partial_value):
    gram_sum = lax.psum(partial_value.astype(jnp.bfloat16), "narrow")
    square = jnp.einsum("cmk,ckn->cmn", gram_sum, gram_sum, preferred_element_type=jnp.float32)
    polynomial = (coef_b * gram_sum.astype(jnp.float32) + coef_c * square).astype(jnp.bfloat16)
    return jnp.einsum("cmk,ckn->cmn", polynomial, current, preferred_element_type=jnp.float32)


def newton_schulz(current):
    result = current.astype(jnp.float32)
    for iteration in range(ITERS):
        partial_value = jnp.einsum(
            "cmk,cnk->cmn", current, current, preferred_element_type=jnp.float32
        )
        product_bx = polynomial_times(current, partial_value)
        result = coef_a * current.astype(jnp.float32) + product_bx
        if iteration + 1 < ITERS:
            current = result.astype(jnp.bfloat16)
    updates = (math.sqrt(D) * result).astype(jnp.bfloat16)
    update_values = updates.astype(jnp.float32)
    update_squares = lax.psum(jnp.sum(update_values * update_values, axis=(1, 2)), "narrow")
    return (updates[None], (update_squares / (KV_OUT * D))[None])


def orthogonalize(slot_block):
    directions = slot_block[0]
    square_sums = lax.psum(jnp.sum(directions * directions, axis=(1, 2)), "narrow")
    current = (directions / (jnp.sqrt(square_sums)[:, None, None] + norm_eps)).astype(jnp.bfloat16)
    return newton_schulz(current)


def on_device(grads, momentum, owners, norm_grads, norm_params, adam_m, adam_v):
    grad_values = grads.astype(jnp.float32)
    momentum_new = muon_beta * momentum + grad_values
    direction = grad_values + muon_beta * momentum_new
    groups = lax.axis_size("wide")
    matrix_count = owners.shape[0]
    matrix_ids = jnp.arange(matrix_count, dtype=jnp.int32)
    capacity = -(-matrix_count // groups)
    slot_of = matrix_ids % groups * capacity + matrix_ids // groups
    slot_total = groups * capacity
    slot_match = slot_of[None, :] == jnp.arange(slot_total, dtype=jnp.int32)[:, None]
    source = jnp.sum(jnp.where(slot_match, matrix_ids[None, :], 0), axis=1) + jnp.where(
        jnp.any(slot_match, axis=1), 0, matrix_count
    )
    row_count = direction.shape[1]
    col_count = direction.shape[2]
    padded = jnp.concatenate([direction, jnp.zeros((1, row_count, col_count), jnp.float32)], axis=0)
    outgoing = jnp.take(padded, source, axis=0).reshape(groups, capacity, row_count, col_count)
    updates, slot_loads = orthogonalize(
        lax.all_to_all(outgoing, "wide", split_axis=0, concat_axis=2, tiled=True)
    )
    returned = lax.all_to_all(updates, "wide", split_axis=2, concat_axis=0, tiled=True)
    arrived = returned.reshape(slot_total, row_count, col_count)
    muon_update = jnp.take(arrived, slot_of, axis=0)
    own_group = lax.axis_index("wide")
    computed_here = matrix_ids % groups == own_group
    local_loads = jnp.where(computed_here, jnp.take(slot_loads[0], matrix_ids // groups), 0.0)
    matrix_loads = lax.psum(local_loads, "wide")
    owner_load = jnp.sum(jnp.where(owners == own_group, matrix_loads, 0.0)).reshape(1)
    adam_m_new = adam_first * adam_m + (1.0 - adam_first) * norm_grads
    adam_v_new = adam_second * adam_v + (1.0 - adam_second) * norm_grads * norm_grads
    corrected = adam_m_new / first_fix / (jnp.sqrt(adam_v_new / second_fix) + adam_eps)
    norm_params_new = norm_params - adam_rate * corrected
    return (muon_update, momentum_new, owner_load, norm_params_new, adam_m_new, adam_v_new)


def solution(mesh):
    return jax.shard_map(
        on_device,
        mesh=mesh,
        in_specs=(
            P(None, "wide", "narrow"),
            P(None, "wide", "narrow"),
            P(),
            P("narrow", "wide"),
            P("narrow", "wide"),
            P("narrow", "wide"),
            P("narrow", "wide"),
        ),
        out_specs=(
            P(None, "wide", "narrow"),
            P(None, "wide", "narrow"),
            P("wide"),
            P("narrow", "wide"),
            P("narrow", "wide"),
            P("narrow", "wide"),
        ),
        check_vma=False,
    )
```

profile of v0, /device:TPU:0, one launch (start us, length us, event | category | flops | bytes accessed | tf_op | source)
XLA Modules:
  0.0 207.1 jit_solution(12475647661025235217)
XLA Ops:
  7.5 3.5 %convert_add_fusion = (f32[14,32,1024]{2,1,0:T(8,128)S(1)}, f32[14,32,1024]{2,1,0:T(8,128)}) fusion(bf16[14,32,1024]{2,1,0:T(8,128)(2,1)} %param.7, f32[14,32,1024]{2,1,0:T(8,128)} %param.8), kind=kLoop, calls=%fused_computation.2 | loop fusion | flops 2293760 | bytes 6422528 | tf_op jit(solution)/shard_map/add | solution.py:59
  11.2 2.0 gather_fusion
  13.3 1.8 bitcast_select_fusion
  15.1 57.0 %all_to_all.8 = f32[16,1,32,1024]{3,2,1,0:T(8,128)S(1)} all-to-all(f32[16,1,32,1024]{3,2,1,0:T(8,128)S(1)} %bitcast_select_fusion), channel_id=1, replica_groups=mesh['wide'=16,'narrow'=2] {'wide'}, dimensions={0} | all-to-all | bytes 4194304 | tf_op jit(solution)/shard_map/all_to_all | solution.py:75
  72.1 1.1 multiply_reduce_fusion.1
  73.2 3.1 %psum.35 = f32[1]{0:T(128)} all-reduce(f32[1]{0:T(128)} %bitcast.3), channel_id=1, replica_groups=mesh['wide'=16,'narrow'=2] {'narrow'}, use_global_device_ids=true, to_apply=%region_3.4 | all-reduce | flops 1 | bytes 8 | tf_op jit(solution)/shard_map/psum | solution.py:51
  77.0 1.7 convert_multiply_fusion
  78.7 1.5 fusion.7
  80.5 16.9 %all-reduce.4.cloned.1.call-done = bf16[1,512,512]{2,1,0:T(8,128)(2,1)} async-done(((bf16[1,512,512]{2,1,0:T(8,128)(2,1)}), bf16[1,512,512]{2,1,0:T(8,128)(2,1)}) %all-reduce.4.cloned.1.call-update) | async-done | bytes 524304 | tf_op jit(solution)/shard_map/psum | solution.py:27
  97.4 3.4 %fusion = bf16[512,1024]{1,0:T(8,128)(2,1)} fusion(f32[16,1,32,1024]{3,2,1,0:T(8,128)S(1)} %copy-done, bf16[512,1024]{1,0:T(8,128)(2,1)S(1)} %bitcast.81, bf16[1,512,512]{2,1,0:T(8,128)(2,1)} %all-reduce.4.cloned.1.call-done), kind=kOutput, calls=%fused_computation.5 | convolution fusion | flops 807665664 | bytes 4718592 | tf_op jit(solution)/shard_map/cmk,ckn->cmn/dot_general | solution.py:30
  100.8 3.2 %fusion.8 = bf16[1,512,512]{2,1,0:T(8,128)(2,1)} fusion(bf16[512,1024]{1,0:T(8,128)(2,1)} %fusion), kind=kOutput, calls=%fused_computation.23 | convolution fusion | flops 537133056 | bytes 1572864 | tf_op jit(solution)/shard_map/cmk,cnk->cmn/dot_general | solution.py:36
  104.0 20.1 %all-reduce.6.cloned.1.call-done = bf16[1,512,512]{2,1,0:T(8,128)(2,1)} async-done(((bf16[1,512,512]{2,1,0:T(8,128)(2,1)}), bf16[1,512,512]{2,1,0:T(8,128)(2,1)}) %all-reduce.6.cloned.1.call-update) | async-done | bytes 524304 | tf_op jit(solution)/shard_map/psum | solution.py:27
  124.1 3.2 %multiply_reduce_fusion = (f32[]{:T(128)}, bf16[512,1024]{1,0:T(8,128)(2,1)S(1)}) fusion(bf16[512,1024]{1,0:T(8,128)(2,1)S(1)} %copy-done.6, bf16[1,512,512]{2,1,0:T(8,128)(2,1)} %all-reduce.6.cloned.1.call-done), kind=kOutput, calls=%fused_computation.7 | convolution fusion | flops 810811392 | bytes 2621444 | tf_op jit(solution)/shard_map/cmk,ckn->cmn/dot_general | solution.py:30
  127.3 1.6 copy.18
  129.5 6.8 %reduce.3 = bf16[512,1024]{1,0:T(8,128)(2,1)S(1)} reduce(bf16[512,1,1,1024]{3,2,1,0:T(2,128)(2,1)S(1)} %bitcast.77, bf16[]{:T(256)} %broadcast.355), dimensions={1,2}, to_apply=%bitcast.75.reduce_sub_computation | reduce | bytes 2097154
  136.3 1.6 reshape.253
  137.9 6.8 %all-to-all-start.1 = ((bf16[16,2,16384]{2,1,0:T(2,128)(2,1)}), bf16[16,2,16384]{2,1,0:T(2,128)(2,1)S(1)}, u32[]{:S(2)}, u32[]{:S(2)}) async-start(bf16[16,2,16384]{2,1,0:T(2,128)(2,1)} %reshape.253), calls=%async_computation.1 | async-start | bytes 2097152 | tf_op jit(solution)/shard_map/all_to_all | solution.py:77
  144.8 0.6 multiply_subtract_fusion
  145.4 3.1 %psum.38 = f32[1]{0:T(128)} all-reduce(f32[1]{0:T(128)} %bitcast.17), channel_id=1, replica_groups=mesh['wide'=16,'narrow'=2] {'narrow'}, use_global_device_ids=true, to_apply=%region_7.8 | all-reduce | flops 1 | bytes 8 | tf_op jit(solution)/shard_map/psum | solution.py:45
  149.2 47.4 %psum.39 = f32[14]{0:T(128)S(1)} all-reduce(f32[14]{0:T(128)S(1)} %compare_select_fusion.5), channel_id=1, replica_groups=mesh['wide'=16,'narrow'=2] {'wide'}, use_global_device_ids=true, to_apply=%region_8.9 | all-reduce | flops 14 | bytes 112 | tf_op jit(solution)/shard_map/psum | solution.py:83
  196.6 0.6 fusion.23
  197.2 1.0 reshape.254
  198.6 0.6 gather_fusion.1
  199.2 1.1 broadcast_select_fusion
  (32 shorter events, 1.8 us)
Async XLA Ops:
  7.2 90.2 %all-reduce.4.cloned.1.call-start = ((), (), s32[]{:S(2)}) async-start(), calls=%async_computation.2 | async-start | bytes 1048576 | tf_op jit(solution)/shard_map/psum | solution.py:27
  78.7 18.7 %copy-start = (f32[16,1,32,1024]{3,2,1,0:T(8,128)S(1)}, f32[16,1,32,1024]{3,2,1,0:T(8,128)}, u32[]{:S(2)}) copy-start(f32[16,1,32,1024]{3,2,1,0:T(8,128)} %get-tuple-element.9) | copy-start | bytes 6291460
  80.3 43.8 %all-reduce.6.cloned.1.call-start = ((), (), s32[]{:S(2)}) async-start(), calls=%async_computation.3 | async-start | bytes 1048576 | tf_op jit(solution)/shard_map/psum | solution.py:27
  100.8 23.3 %copy-start.6 = (bf16[512,1024]{1,0:T(8,128)(2,1)S(1)}, bf16[512,1024]{1,0:T(8,128)(2,1)}, u32[]{:S(2)}) copy-start(bf16[512,1024]{1,0:T(8,128)(2,1)} %fusion) | copy-start | bytes 3145732
  136.2 8.5 %copy-start.1 = (f32[14,128]{1,0:T(8,128)S(1)}, f32[14,128]{1,0:T(8,128)}, u32[]{:S(2)}) copy-start(f32[14,128]{1,0:T(8,128)} %param.11) | copy-start | bytes 21508
  136.3 8.5 %copy-start.2 = (f32[14,128]{1,0:T(8,128)S(1)}, f32[14,128]{1,0:T(8,128)}, u32[]{:S(2)}) copy-start(f32[14,128]{1,0:T(8,128)} %param.10) | copy-start | bytes 21508
  136.3 8.5 %copy-start.3 = (f32[14,128]{1,0:T(8,128)S(1)}, f32[14,128]{1,0:T(8,128)}, u32[]{:S(2)}) copy-start(f32[14,128]{1,0:T(8,128)} %param.12) | copy-start | bytes 21508
  136.3 8.5 %copy-start.4 = (f32[14,128]{1,0:T(8,128)S(1)}, f32[14,128]{1,0:T(8,128)}, u32[]{:S(2)}) copy-start(f32[14,128]{1,0:T(8,128)} %param.13) | copy-start | bytes 21508
  136.3 60.3 %copy-start.5 = (s32[14]{0:T(128)S(1)}, s32[14]{0:T(128)}, u32[]{:S(2)}) copy-start(s32[14]{0:T(128)} %param.9) | copy-start | bytes 172
  137.9 59.3 %all-to-all-start.1 = ((bf16[16,2,16384]{2,1,0:T(2,128)(2,1)}), bf16[16,2,16384]{2,1,0:T(2,128)(2,1)S(1)}, u32[]{:S(2)}, u32[]{:S(2)}) async-start(bf16[16,2,16384]{2,1,0:T(2,128)(2,1)} %reshape.253), calls=%async_computation.1 | async-start | bytes 2097152 | tf_op jit(solution)/shard_map/all_to_all | solution.py:77
Sparse Core Ops, SparseCore 0:
  80.4 16.9 all-reduce.3
  104.1 19.9 all-reduce.5
where the time goes:
time: 208 us; the launch traced here: 207 us
  blocking collectives  111 us (53%)
  waiting for transfers between devices  37 us (18%)
  other arithmetic  17.5 us (8%)
  between operations  15.6 us (8%)
  matrix products  11.3 us (5%)
  local copies, waits for them, and re-layouts  8.1 us (4%)
  starting transfers between devices  7.05 us (3%)
    all_to_all x1, blocking collectives, on_device(): lax.all_to_all(outgoing, 'wide', split_axis=0, concat_axis=2, tiled=True)  57 us
    psum x1, blocking collectives, on_device(): matrix_loads = lax.psum(local_loads, 'wide')  47.4 us
    psum x2, waiting for transfers between devices, polynomial_times(): gram_sum = lax.psum(partial_value.astype(jnp.bfloat16), 'narrow')  37 us
    all_to_all x1, starting transfers between devices, on_device(): lax.all_to_all(updates, 'wide', split_axis=2, concat_axis=0, tiled=True)  6.79 us
    unnamed x1, other arithmetic  6.78 us
    dot_general x2, matrix products, polynomial_times(): jnp.einsum('cmk,ckn->cmn', polynomial, current, preferred_element_type=jn...  6.64 us
    dot_general x2, matrix products, newton_schulz(): jnp.einsum('cmk,cnk->cmn', current, current, preferred_element_type=jnp.f...  4.71 us
  transfers between devices with their start and end apart: 3, of which 2 were waited for; matrix products, arithmetic and copies ran while one was open for 1% of the time, Pallas kernels for 0%

commit v1 on v0

v1 whole, which is shorter than its diff:
```python
import functools
import math

import jax
import jax.numpy as jnp
from jax import lax
from jax.experimental import pallas as pl
from jax.experimental.pallas import tpu as pltpu
from jax.sharding import PartitionSpec as P

D = 2048
KV_OUT = 512

coef_a = 3.4445
coef_b = -4.775
coef_c = 2.0315
muon_beta = 0.95
norm_eps = 1e-07
adam_first = 0.9
adam_second = 0.95
adam_rate = 0.02
adam_eps = 1e-08
first_fix = 1.0 - 0.9**10
second_fix = 1.0 - 0.95**10

MESH = pl.DeviceIdType.MESH
BF16 = jnp.bfloat16
F32 = jnp.float32


def mul(left, right):
    return jnp.dot(left, right, preferred_element_type=F32)


def kernel(
    groups, parts, mats, chunks,
    owners, grads, momentum,
    update, momentum_new, owner_load,
    dirs, blocks, results, grams, traces, halves, load_tile, loads, fresh, ident,
    dir_send, dir_recv, res_send, res_recv, gram_send, gram_recv,
    trace_send, trace_recv, half_send, half_recv, load_send, load_recv, own_sem, mom_sem,
):
    me = lax.axis_index("wide")
    part = lax.axis_index("narrow")
    rows, cols = dirs.shape[1], dirs.shape[2]

    def matrix_of(group):
        matrix = lax.div(group * mats + (groups - 1), groups)
        owned = (lax.div(matrix * groups, mats) == group) & (matrix < mats)
        return jnp.minimum(matrix, mats - 1), owned

    my_matrix, is_owner = matrix_of(me)

    def group_at(step):
        return lax.rem(me + step, groups)

    barrier = pltpu.get_barrier_semaphore()

    @pl.loop(1, groups)
    def _(step):
        pl.semaphore_signal(barrier, inc=1, device_id=(group_at(step), part), device_id_type=MESH)

    for step in range(1, parts):
        peer = lax.rem(part + step, parts)
        pl.semaphore_signal(barrier, inc=1, device_id=(me, peer), device_id_type=MESH)

    @pl.loop(0, mats)
    def _(matrix):
        grad_values = grads[matrix].astype(F32)
        new = muon_beta * momentum[matrix] + grad_values
        fresh[matrix] = new
        dirs[matrix] = (grad_values + muon_beta * new).astype(BF16)

    pl.semaphore_wait(barrier, groups - 1 + parts - 1)

    def dir_copy(matrix, group, slot):
        return pltpu.make_async_remote_copy(
            src_ref=dirs.at[matrix], dst_ref=blocks.at[slot],
            send_sem=dir_send.at[matrix], recv_sem=dir_recv.at[slot],
            device_id=(group, part), device_id_type=MESH,
        )

    @pl.loop(0, groups)
    def _(step):
        group = group_at(step + groups // 2)
        matrix, owned = matrix_of(group)

        @pl.when(owned & (group != me))
        def _():
            dir_copy(matrix, group, me).start()

    mom_copy = pltpu.make_async_copy(fresh, momentum_new, mom_sem)
    mom_copy.start()

    def result_copy(group, matrix):
        return pltpu.make_async_remote_copy(
            src_ref=results.at[group], dst_ref=update.at[matrix],
            send_sem=res_send.at[group], recv_sem=res_recv.at[matrix],
            device_id=(group, part), device_id_type=MESH,
        )

    def load_copy(group, matrix):
        return pltpu.make_async_remote_copy(
            src_ref=load_tile, dst_ref=loads.at[matrix],
            send_sem=load_send.at[group], recv_sem=load_recv.at[matrix],
            device_id=(group, part), device_id_type=MESH,
        )

    def peer_copy(buffer, peer, slot, send, recv):
        return pltpu.make_async_remote_copy(
            src_ref=buffer.at[slot], dst_ref=buffer.at[slot],
            send_sem=send.at[peer], recv_sem=recv.at[slot],
            device_id=(me, peer), device_id_type=MESH,
        )

    @pl.when(is_owner)
    def _():
        blocks[me] = dirs[my_matrix]
        row_ids = lax.broadcasted_iota(jnp.int32, (KV_OUT, KV_OUT), 0)
        col_ids = lax.broadcasted_iota(jnp.int32, (KV_OUT, KV_OUT), 1)

        @pl.loop(1, groups)
        def _(step):
            source = group_at(step)
            dir_copy(my_matrix, me, source).wait_recv()

        matrix = blocks[...].reshape(KV_OUT, cols)
        partial_value = lax.dot_general(
            matrix, matrix, (((1,), (1,)), ((), ())), preferred_element_type=F32
        )
        grams[part] = partial_value.astype(BF16)
        squares = jnp.sum(jnp.where(row_ids == col_ids, partial_value, 0.0))
        traces[part] = jnp.full((8, 128), squares, F32)
        for step in range(1, parts):
            peer = lax.rem(part + step, parts)
            peer_copy(grams, peer, part, gram_send, gram_recv).start()
            peer_copy(traces, peer, part, trace_send, trace_recv).start()
        for step in range(1, parts):
            peer = lax.rem(part + step, parts)
            peer_copy(grams, peer, peer, gram_send, gram_recv).wait_recv()
            peer_copy(traces, peer, peer, trace_send, trace_recv).wait_recv()
        gram_sum = jnp.sum(grams[...].astype(F32), axis=0)
        square_sum = jnp.sum(traces[...], axis=0)[0:1, 0:1]
        scale = 1.0 / (jnp.sqrt(square_sum) + norm_eps)
        gram = (gram_sum * scale * scale).astype(BF16)
        gram_wide = gram.astype(F32)
        poly = coef_b * gram_wide + coef_c * mul(gram, gram)
        poly_first = poly.astype(BF16)
        mixed = mul(poly_first, gram)
        next_gram = (
            (coef_a * coef_a) * gram_wide
            + (2.0 * coef_a) * mixed
            + mul(mixed.astype(BF16), poly_first)
        ).astype(BF16)
        poly_second = (
            coef_b * next_gram.astype(F32) + coef_c * mul(next_gram, next_gram)
        )
        total = (
            coef_a * (poly_first.astype(F32) + poly_second)
            + mul(poly_second.astype(BF16), poly_first)
        )
        ident[...] = total.astype(BF16).reshape(ident.shape)

        out_scale = scale * math.sqrt(D)
        per_chunk = groups // chunks
        chunk_rows = KV_OUT // chunks
        my_chunk = lax.div(me, per_chunk)

        def chunk_body(step, square_total):
            chunk = lax.rem(my_chunk + step + chunks // 2, chunks)
            first = chunk * per_chunk
            mine = blocks[pl.ds(first, per_chunk)].reshape(chunk_rows, cols)
            factor = ident[pl.ds(first, per_chunk)].reshape(chunk_rows, KV_OUT)
            values = (coef_a * coef_a) * mine.astype(F32) + mul(
                factor, blocks[...].reshape(KV_OUT, cols)
            )
            rounded = (out_scale * values).astype(BF16)
            results[pl.ds(first, per_chunk)] = rounded.reshape(per_chunk, rows, cols)

            @pl.loop(0, per_chunk)
            def _(member):
                group = first + lax.rem(me + member, per_chunk)

                @pl.when(group != me)
                def _():
                    result_copy(group, my_matrix).start()

                @pl.when(group == me)
                def _():
                    pltpu.make_async_copy(results.at[me], update.at[my_matrix], own_sem).start()

            wide = rounded.astype(F32)
            return square_total + jnp.sum(wide * wide)

        square_total = lax.fori_loop(0, chunks, chunk_body, jnp.zeros((), F32))
        halves[part] = jnp.full((8, 128), square_total, F32)
        for step in range(1, parts):
            peer = lax.rem(part + step, parts)
            peer_copy(halves, peer, part, half_send, half_recv).start()
        for step in range(1, parts):
            peer = lax.rem(part + step, parts)
            peer_copy(halves, peer, peer, half_send, half_recv).wait_recv()
        load_tile[...] = jnp.sum(halves[...], axis=0) / (KV_OUT * D)
        loads[my_matrix] = load_tile[...]

        @pl.loop(1, groups)
        def _(step):
            load_copy(group_at(step), my_matrix).start()

        for step in range(1, parts):
            peer = lax.rem(part + step, parts)
            peer_copy(grams, peer, part, gram_send, gram_recv).wait_send()
            peer_copy(traces, peer, part, trace_send, trace_recv).wait_send()
            peer_copy(halves, peer, part, half_send, half_recv).wait_send()

        @pl.loop(1, groups)
        def _(step):
            group = group_at(step)
            result_copy(group, my_matrix).wait_send()
            load_copy(group, my_matrix).wait_send()

        pltpu.make_async_copy(results.at[me], update.at[my_matrix], own_sem).wait()

    @pl.loop(1, groups)
    def _(step):
        group = group_at(step)
        matrix, owned = matrix_of(group)

        @pl.when(owned)
        def _():
            dir_copy(matrix, group, me).wait_send()
            result_copy(me, matrix).wait_recv()
            load_copy(me, matrix).wait_recv()

    total_load = jnp.zeros((8, 128), F32)
    for matrix in range(mats):
        total_load = total_load + jnp.where(owners[matrix] == me, 1.0, 0.0) * loads[matrix]
    owner_load[...] = total_load
    mom_copy.wait()


def on_device(groups, parts, grads, momentum, owners, norm_grads, norm_params, adam_m, adam_v):
    mats, rows, cols = grads.shape
    dma = pltpu.SemaphoreType.DMA
    vmem = pl.BlockSpec(memory_space=pltpu.VMEM)
    hbm = pl.BlockSpec(memory_space=pl.ANY)
    update, momentum_new, load_block = pl.pallas_call(
        functools.partial(kernel, groups, parts, mats, 4),
        out_shape=(
            jax.ShapeDtypeStruct((mats, rows, cols), BF16),
            jax.ShapeDtypeStruct((mats, rows, cols), F32),
            jax.ShapeDtypeStruct((8, 128), F32),
        ),
        in_specs=[pl.BlockSpec(memory_space=pltpu.SMEM), vmem, vmem],
        out_specs=(hbm, hbm, vmem),
        scratch_shapes=[
            pltpu.VMEM((mats, rows, cols), BF16),
            pltpu.VMEM((groups, rows, cols), BF16),
            pltpu.VMEM((groups, rows, cols), BF16),
            pltpu.VMEM((parts, KV_OUT, KV_OUT), BF16),
            pltpu.VMEM((parts, 8, 128), F32),
            pltpu.VMEM((parts, 8, 128), F32),
            pltpu.VMEM((8, 128), F32),
            pltpu.VMEM((mats, 8, 128), F32),
            pltpu.VMEM((mats, rows, cols), F32),
            pltpu.VMEM((groups, rows, KV_OUT), BF16),
            dma((mats,)), dma((groups,)), dma((groups,)), dma((mats,)),
            dma((parts,)), dma((parts,)), dma((parts,)), dma((parts,)),
            dma((parts,)), dma((parts,)), dma((groups,)), dma((mats,)),
            dma, dma,
        ],
        compiler_params=pltpu.CompilerParams(
            collective_id=0, has_side_effects=True, vmem_limit_bytes=48 * 1024 * 1024
        ),
    )(owners, grads, momentum)
    adam_m_new = adam_first * adam_m + (1.0 - adam_first) * norm_grads
    adam_v_new = adam_second * adam_v + (1.0 - adam_second) * norm_grads * norm_grads
    corrected = adam_m_new / first_fix / (jnp.sqrt(adam_v_new / second_fix) + adam_eps)
    norm_params_new = norm_params - adam_rate * corrected
    return (update, momentum_new, load_block[0, 0:1], norm_params_new, adam_m_new, adam_v_new)


def solution(mesh):
    return jax.shard_map(
        functools.partial(on_device, mesh.shape["wide"], mesh.shape["narrow"]),
        mesh=mesh,
        in_specs=(
            P(None, "wide", "narrow"),
            P(None, "wide", "narrow"),
            P(),
            P("narrow", "wide"),
            P("narrow", "wide"),
            P("narrow", "wide"),
            P("narrow", "wide"),
        ),
        out_specs=(
            P(None, "wide", "narrow"),
            P(None, "wide", "narrow"),
            P("wide"),
            P("narrow", "wide"),
            P("narrow", "wide"),
            P("narrow", "wide"),
        ),
        check_vma=False,
    )
```

time: 208 us -> 65.8 us (0.32)
  blocking collectives: 111 us -> 0 us
  Pallas kernels: 0 us -> 57.5 us
  waiting for transfers between devices: 37 us -> 0 us
  other arithmetic: 17.5 us -> 0.62 us
  between operations: 15.6 us -> 0.66 us
  matrix products: 11.3 us -> 0 us
  starting transfers between devices: 7.05 us -> 0 us
  local copies, waits for them, and re-layouts: 8.1 us -> 6 us
    pallas_call x0 -> x1, Pallas kernels: none -> 57.5 us  [on_device(): pl.pallas_call(functools.partial(kernel, groups, parts, mats, 4), out_sha...]
    all_to_all x1 -> x0, blocking collectives: 57 us -> none  [on_device(): lax.all_to_all(outgoing, 'wide', split_axis=0, concat_axis=2, tiled=True)]
    psum x3 -> x0, blocking collectives: 53.6 us -> none  [the longest x1 47.4 us: on_device(): matrix_loads = lax.psum(local_loads, 'wide')]
    psum x2 -> x0, waiting for transfers between devices: 37 us -> none  [polynomial_times(): gram_sum = lax.psum(partial_value.astype(jnp.bfloat16), 'narrow')]
    dot_general x4 -> x0, matrix products: 11.3 us -> none  [the longest x2 6.64 us: polynomial_times(): jnp.einsum('cmk,ckn->cmn', polynomial, current, preferred_element_type=jn...]
    all_to_all x1 -> x0, starting transfers between devices: 6.79 us -> none  [on_device(): lax.all_to_all(updates, 'wide', split_axis=2, concat_axis=0, tiled=True)]
    unnamed x1 -> x0, other arithmetic: 6.78 us -> none
    add x2 -> x0, other arithmetic: 3.48 us -> none  [the longest x1 3.48 us: on_device(): direction = grad_values + muon_beta * momentum_new]
  transfers between devices with their start and end apart: 3 -> 0, of which waited for: 2 -> 0; matrix products, arithmetic and copies ran while one was open for 1% -> 0% of each run, Pallas kernels for 0% -> 0%
where the time goes in v1:
time: 65.8 us; the launch traced here: 64.8 us
  Pallas kernels  57.5 us (87%)
  local copies, waits for them, and re-layouts  6 us (9%)
  between operations  0.66 us (1%)
    pallas_call x1, Pallas kernels, on_device(): pl.pallas_call(functools.partial(kernel, groups, parts, mats, 4), out_sha...  57.5 us
    unnamed x16, local copies, waits for them, and re-layouts  5.49 us

profile of v1, /device:TPU:0, one launch (start us, length us, event | category | flops | bytes accessed | tf_op | source)
XLA Modules:
  0.0 64.8 jit_solution(2817793305845237813)
XLA Ops:
  0.6 0.0 copy-start
  0.6 1.5 %copy-done = f32[14,32,1024]{2,1,0:T(8,128)S(1)} copy-done((f32[14,32,1024]{2,1,0:T(8,128)S(1)}, f32[14,32,1024]{2,1,0:T(8,128)}, u32[]{:S(2)}) %copy-start) | copy-done | bytes 1835032
  2.1 0.0 copy-start.1
  2.1 1.2 %copy-done.1 = bf16[14,32,1024]{2,1,0:T(8,128)(2,1)S(1)} copy-done((bf16[14,32,1024]{2,1,0:T(8,128)(2,1)S(1)}, bf16[14,32,1024]{2,1,0:T(8,128)(2,1)}, u32[]{:S(2)}) %copy-start.1) | copy-done | bytes 917528
  3.3 0.0 copy-start.2
  3.3 0.7 %copy-done.2 = s32[14]{0:T(128)S(1)} copy-done((s32[14]{0:T(128)S(1)}, s32[14]{0:T(128)}, u32[]{:S(2)}) %copy-start.2) | copy-done | bytes 80
  4.0 0.0 copy-start.3
  4.0 0.0 copy-start.4
  4.0 0.0 copy-start.5
  4.0 0.0 copy-start.6
  4.0 57.5 %shard_map.118 = (bf16[14,32,1024]{2,1,0:T(8,128)(2,1)S(1)}, f32[14,32,1024]{2,1,0:T(8,128)S(1)}, f32[8,128]{1,0:T(8,128)S(1)}) custom-call(s32[14]{0:T(128)S(1)} %copy-done.2, bf16[14,32,1024]{2,1,0:T(8,128)(2,1)S(1)} %copy-done.1, f32[14,32,1024]{2,1,0:T(8,128)S(1)} %copy-done), custom_call_target="tpu_custom_call" | custom-call | tf_op jit(solution)/shard_map/pallas_call | solution.py:247
  61.5 0.5 slice.3
  62.0 0.0 copy-done.3
  62.0 0.0 copy-done.4
  62.0 0.0 copy-done.5
  62.0 0.0 copy-done.6
  62.0 0.6 multiply_subtract_fusion
  62.7 0.9 %copy.15 = bf16[14,32,1024]{2,1,0:T(8,128)(2,1)} copy(bf16[14,32,1024]{2,1,0:T(8,128)(2,1)S(1)} %get-tuple-element.21) | data formatting | bytes 1835008
  63.6 1.2 %copy.16 = f32[14,32,1024]{2,1,0:T(8,128)} copy(f32[14,32,1024]{2,1,0:T(8,128)S(1)} %get-tuple-element.22) | data formatting | bytes 3670016
Async XLA Ops:
  0.6 1.5 %copy-start = (f32[14,32,1024]{2,1,0:T(8,128)S(1)}, f32[14,32,1024]{2,1,0:T(8,128)}, u32[]{:S(2)}) copy-start(f32[14,32,1024]{2,1,0:T(8,128)} %momentum.1) | copy-start | bytes 5505028
  2.1 1.2 %copy-start.1 = (bf16[14,32,1024]{2,1,0:T(8,128)(2,1)S(1)}, bf16[14,32,1024]{2,1,0:T(8,128)(2,1)}, u32[]{:S(2)}) copy-start(bf16[14,32,1024]{2,1,0:T(8,128)(2,1)} %grads.1) | copy-start | bytes 2752516
  3.3 0.7 %copy-start.2 = (s32[14]{0:T(128)S(1)}, s32[14]{0:T(128)}, u32[]{:S(2)}) copy-start(s32[14]{0:T(128)} %owners.1) | copy-start | bytes 172
  4.0 58.1 %copy-start.3 = (f32[14,128]{1,0:T(8,128)S(1)}, f32[14,128]{1,0:T(8,128)}, u32[]{:S(2)}) copy-start(f32[14,128]{1,0:T(8,128)} %param.11) | copy-start | bytes 21508
  4.0 58.1 %copy-start.4 = (f32[14,128]{1,0:T(8,128)S(1)}, f32[14,128]{1,0:T(8,128)}, u32[]{:S(2)}) copy-start(f32[14,128]{1,0:T(8,128)} %param.10) | copy-start | bytes 21508
  4.0 58.1 %copy-start.5 = (f32[14,128]{1,0:T(8,128)S(1)}, f32[14,128]{1,0:T(8,128)}, u32[]{:S(2)}) copy-start(f32[14,128]{1,0:T(8,128)} %param.12) | copy-start | bytes 21508
  4.0 58.1 %copy-start.6 = (f32[14,128]{1,0:T(8,128)S(1)}, f32[14,128]{1,0:T(8,128)}, u32[]{:S(2)}) copy-start(f32[14,128]{1,0:T(8,128)} %param.13) | copy-start | bytes 21508

commit v2 on v1

--- a/solution.py
+++ b/solution.py
@@ -34,11 +34,12 @@
 
 def kernel(
     groups, parts, mats, chunks,
-    owners, grads, momentum,
+    owners_hbm, grads_hbm, momentum_hbm,
     update, momentum_new, owner_load,
     dirs, blocks, results, grams, traces, halves, load_tile, loads, fresh, ident,
     dir_send, dir_recv, res_send, res_recv, gram_send, gram_recv,
     trace_send, trace_recv, half_send, half_recv, load_send, load_recv, own_sem, mom_sem,
+    owners, grads, momentum, owners_sem, grads_sem, momentum_sem,
 ):
     me = lax.axis_index("wide")
     part = lax.axis_index("narrow")
@@ -54,6 +55,41 @@
     def group_at(step):
         return lax.rem(me + step, groups)
 
+    def loads_of(matrix):
+        return (
+            pltpu.make_async_copy(grads_hbm.at[matrix], grads.at[matrix], grads_sem.at[matrix]),
+            pltpu.make_async_copy(
+                momentum_hbm.at[matrix], momentum.at[matrix], momentum_sem.at[matrix]
+            ),
+        )
+
+    half = groups // 2
+
+    def member_of(wave, step):
+        place = lax.rem(me + step + half // 2, half)
+        if wave == 0:
+            return place + jnp.where(place < half // 2, 0, half)
+        return place + half // 2
+
+    def on_member(wave, step, body):
+        group = member_of(wave, step)
+        matrix, owned = matrix_of(group)
+
+        @pl.when(owned)
+        def _():
+            body(matrix, group)
+
+    def each_owner(wave, body):
+        @pl.loop(0, half)
+        def _(step):
+            on_member(wave, step, body)
+
+    def fetch(matrix, group):
+        for copy in loads_of(matrix):
+            copy.start()
+
+    owners_copy = pltpu.make_async_copy(owners_hbm, owners, owners_sem)
+    owners_copy.start()
     barrier = pltpu.get_barrier_semaphore()
 
     @pl.loop(1, groups)
@@ -64,13 +100,8 @@
         peer = lax.rem(part + step, parts)
         pl.semaphore_signal(barrier, inc=1, device_id=(me, peer), device_id_type=MESH)
 
-    @pl.loop(0, mats)
-    def _(matrix):
-        grad_values = grads[matrix].astype(F32)
-        new = muon_beta * momentum[matrix] + grad_values
-        fresh[matrix] = new
-        dirs[matrix] = (grad_values + muon_beta * new).astype(BF16)
-
+    each_owner(0, fetch)
+    each_owner(1, fetch)
     pl.semaphore_wait(barrier, groups - 1 + parts - 1)
 
     def dir_copy(matrix, group, slot):
@@ -80,14 +111,46 @@
             device_id=(group, part), device_id_type=MESH,
         )
 
-    @pl.loop(0, groups)
-    def _(step):
-        group = group_at(step + groups // 2)
-        matrix, owned = matrix_of(group)
-
-        @pl.when(owned & (group != me))
+    def direct(matrix, group):
+        for copy in loads_of(matrix):
+            copy.wait()
+        grad_values = grads[matrix].astype(F32)
+        new = muon_beta * momentum[matrix] + grad_values
+        fresh[matrix] = new
+        dirs[matrix] = (grad_values + muon_beta * new).astype(BF16)
+
+    def direct_and_send(matrix, group):
+        direct(matrix, group)
+
+        @pl.when(group != me)
         def _():
             dir_copy(matrix, group, me).start()
+
+    def drain(matrix, group):
+        @pl.when(group != me)
+        def _():
+            dir_copy(matrix, group, me).wait_send()
+
+    def send(matrix, group):
+        @pl.when(group != me)
+        def _():
+            dir_copy(matrix, group, me).start()
+
+    each_owner(0, direct_and_send)
+    each_owner(1, direct)
+    @pl.loop(0, half // 2)
+    def _(step):
+        on_member(1, step, send)
+
+    @pl.loop(0, half // 2)
+    def _(step):
+        on_member(0, step, drain)
+        on_member(1, step + half // 2, send)
+
+    @pl.loop(half // 2, half)
+    def _(step):
+        on_member(0, step, drain)
+
 
     mom_copy = pltpu.make_async_copy(fresh, momentum_new, mom_sem)
     mom_copy.start()
@@ -221,6 +284,8 @@
 
         pltpu.make_async_copy(results.at[me], update.at[my_matrix], own_sem).wait()
 
+    each_owner(1, drain)
+
     @pl.loop(1, groups)
     def _(step):
         group = group_at(step)
@@ -228,10 +293,10 @@
 
         @pl.when(owned)
         def _():
-            dir_copy(matrix, group, me).wait_send()
             result_copy(me, matrix).wait_recv()
             load_copy(me, matrix).wait_recv()
 
+    owners_copy.wait()
     total_load = jnp.zeros((8, 128), F32)
     for matrix in range(mats):
         total_load = total_load + jnp.where(owners[matrix] == me, 1.0, 0.0) * loads[matrix]
@@ -251,7 +316,7 @@
             jax.ShapeDtypeStruct((mats, rows, cols), F32),
             jax.ShapeDtypeStruct((8, 128), F32),
         ),
-        in_specs=[pl.BlockSpec(memory_space=pltpu.SMEM), vmem, vmem],
+        in_specs=[pl.BlockSpec(memory_space=pltpu.HBM)] * 3,
         out_specs=(hbm, hbm, vmem),
         scratch_shapes=[
             pltpu.VMEM((mats, rows, cols), BF16),
@@ -268,9 +333,13 @@
             dma((parts,)), dma((parts,)), dma((parts,)), dma((parts,)),
             dma((parts,)), dma((parts,)), dma((groups,)), dma((mats,)),
             dma, dma,
+            pltpu.SMEM((mats,), jnp.int32),
+            pltpu.VMEM((mats, rows, cols), BF16),
+            pltpu.VMEM((mats, rows, cols), F32),
+            dma, dma((mats,)), dma((mats,)),
         ],
         compiler_params=pltpu.CompilerParams(
-            collective_id=0, has_side_effects=True, vmem_limit_bytes=48 * 1024 * 1024
+            collective_id=0, has_side_effects=True, vmem_limit_bytes=60 * 1024 * 1024
         ),
     )(owners, grads, momentum)
     adam_m_new = adam_first * adam_m + (1.0 - adam_first) * norm_grads

time: 65.8 us -> 62.4 us (0.948)
  Pallas kernels: 57.5 us -> 56 us
  local copies, waits for them, and re-layouts: 6 us -> 4.74 us
    unnamed x16 -> x12, local copies, waits for them, and re-layouts: 5.49 us -> 3.42 us
    pallas_call x1, Pallas kernels: 57.5 us -> 56 us  [on_device(): pl.pallas_call(functools.partial(kernel, groups, parts, mats, 4), out_sha...]
    slice x1, local copies, waits for them, and re-layouts: 0.51 us -> 1.33 us  [on_device(): load_block[0, 0:1]]
where the time goes in v2:
time: 62.4 us; the launch traced here: 62.1 us
  Pallas kernels  56 us (90%)
  local copies, waits for them, and re-layouts  4.74 us (8%)
  between operations  0.7 us (1%)
    pallas_call x1, Pallas kernels, on_device(): pl.pallas_call(functools.partial(kernel, groups, parts, mats, 4), out_sha...  56 us
    unnamed x12, local copies, waits for them, and re-layouts  3.42 us
    slice x1, local copies, waits for them, and re-layouts, on_device(): load_block[0, 0:1]  1.33 us

profile of v2, /device:TPU:0, one launch (start us, length us, event | category | flops | bytes accessed | tf_op | source)
XLA Modules:
  0.0 62.1 jit_solution(16905300606991017488)
XLA Ops:
  0.6 0.0 copy-start.2
  0.6 0.0 copy-start.1
  0.7 0.0 copy-start.3
  0.7 0.0 copy-start.4
  0.7 56.0 %shard_map.118 = (bf16[14,32,1024]{2,1,0:T(8,128)(2,1)}, f32[14,32,1024]{2,1,0:T(8,128)}, f32[8,128]{1,0:T(8,128)}) custom-call(s32[14]{0:T(128)} %owners_hbm.1, bf16[14,32,1024]{2,1,0:T(8,128)(2,1)} %grads_hbm.1, f32[14,32,1024]{2,1,0:T(8,128)} %momentum_hbm.1), custom_call_target="tpu_custom_call" | custom-call | tf_op jit(solution)/shard_map/pallas_call | solution.py:312
  56.7 0.0 copy-start
  56.7 1.3 %slice.3 = f32[1,1]{1,0:T(1,128)} slice(f32[8,128]{1,0:T(8,128)} %get-tuple-element.11), slice={[0:1], [0:1]} | slice | bytes 8 | tf_op jit(solution)/shard_map/slice | solution.py:349
  58.0 0.0 copy-done.2
  58.0 0.0 copy-done.1
  58.0 0.0 copy-done.3
  58.0 0.0 copy-done.4
  58.0 0.6 %multiply_subtract_fusion = (f32[14,128]{1,0:T(8,128)}, f32[14,128]{1,0:T(8,128)}, f32[14,128]{1,0:T(8,128)}) fusion(f32[14,128]{1,0:T(8,128)S(1)} %copy-done.1, f32[14,128]{1,0:T(8,128)S(1)} %copy-done.2, f32[14,128]{1,0:T(8,128)S(1)} %copy-done.3, f32[14,128]{1,0:T(8,128)S(1)} %copy-done.4), kind=kLoop, calls=%fused_computation.2 | loop fusion | flops 23296 | bytes 50176 | tf_op jit(solution)/shard_map/sub | solution.py:348
  58.7 2.2 %copy.15 = bf16[14,32,1024]{2,1,0:T(8,128)(2,1)} copy(bf16[14,32,1024]{2,1,0:T(8,128)(2,1)} %get-tuple-element.21) | data formatting | bytes 1835008
  60.8 0.0 copy-done
  60.8 1.2 %copy.16 = f32[14,32,1024]{2,1,0:T(8,128)} copy(f32[14,32,1024]{2,1,0:T(8,128)S(1)} %copy-done) | data formatting | bytes 3670016
Async XLA Ops:
  0.6 57.4 %copy-start.2 = (f32[14,128]{1,0:T(8,128)S(1)}, f32[14,128]{1,0:T(8,128)}, u32[]{:S(2)}) copy-start(f32[14,128]{1,0:T(8,128)} %param.10) | copy-start | bytes 21508
  0.6 57.4 %copy-start.1 = (f32[14,128]{1,0:T(8,128)S(1)}, f32[14,128]{1,0:T(8,128)}, u32[]{:S(2)}) copy-start(f32[14,128]{1,0:T(8,128)} %param.11) | copy-start | bytes 21508
  0.7 57.4 %copy-start.3 = (f32[14,128]{1,0:T(8,128)S(1)}, f32[14,128]{1,0:T(8,128)}, u32[]{:S(2)}) copy-start(f32[14,128]{1,0:T(8,128)} %param.12) | copy-start | bytes 21508
  0.7 57.4 %copy-start.4 = (f32[14,128]{1,0:T(8,128)S(1)}, f32[14,128]{1,0:T(8,128)}, u32[]{:S(2)}) copy-start(f32[14,128]{1,0:T(8,128)} %param.13) | copy-start | bytes 21508
  56.7 4.2 %copy-start = (f32[14,32,1024]{2,1,0:T(8,128)S(1)}, f32[14,32,1024]{2,1,0:T(8,128)}, u32[]{:S(2)}) copy-start(f32[14,32,1024]{2,1,0:T(8,128)} %get-tuple-element.22) | copy-start | bytes 5505028

commit v3 on v2

--- a/solution.py
+++ b/solution.py
@@ -302,6 +302,27 @@
         total_load = total_load + jnp.where(owners[matrix] == me, 1.0, 0.0) * loads[matrix]
     owner_load[...] = total_load
     mom_copy.wait()
+
+
+def finish(
+    update, momentum, load_block, norm_grads, norm_params, adam_m, adam_v,
+    update_out, momentum_out, load_out, params_out, adam_m_out, adam_v_out,
+    update_sem, momentum_sem,
+):
+    momentum_copy = pltpu.make_async_copy(momentum, momentum_out, momentum_sem)
+    update_copy = pltpu.make_async_copy(update, update_out, update_sem)
+    momentum_copy.start()
+    update_copy.start()
+    grad = norm_grads[...]
+    adam_m_new = adam_first * adam_m[...] + (1.0 - adam_first) * grad
+    adam_v_new = adam_second * adam_v[...] + (1.0 - adam_second) * grad * grad
+    corrected = adam_m_new / first_fix / (jnp.sqrt(adam_v_new / second_fix) + adam_eps)
+    params_out[...] = norm_params[...] - adam_rate * corrected
+    adam_m_out[...] = adam_m_new
+    adam_v_out[...] = adam_v_new
+    load_out[0] = load_block[0, 0]
+    momentum_copy.wait()
+    update_copy.wait()
 
 
 def on_device(groups, parts, grads, momentum, owners, norm_grads, norm_params, adam_m, adam_v):
@@ -342,11 +363,20 @@
             collective_id=0, has_side_effects=True, vmem_limit_bytes=60 * 1024 * 1024
         ),
     )(owners, grads, momentum)
-    adam_m_new = adam_first * adam_m + (1.0 - adam_first) * norm_grads
-    adam_v_new = adam_second * adam_v + (1.0 - adam_second) * norm_grads * norm_grads
-    corrected = adam_m_new / first_fix / (jnp.sqrt(adam_v_new / second_fix) + adam_eps)
-    norm_params_new = norm_params - adam_rate * corrected
-    return (update, momentum_new, load_block[0, 0:1], norm_params_new, adam_m_new, adam_v_new)
+    norm_shape = jax.ShapeDtypeStruct(norm_grads.shape, F32)
+    update, momentum_new, owner_load, norm_params_new, adam_m_new, adam_v_new = pl.pallas_call(
+        finish,
+        out_shape=(
+            jax.ShapeDtypeStruct(update.shape, BF16),
+            jax.ShapeDtypeStruct(momentum_new.shape, F32),
+            jax.ShapeDtypeStruct((1,), F32),
+            norm_shape, norm_shape, norm_shape,
+        ),
+        in_specs=[vmem] * 7,
+        out_specs=(hbm, hbm, pl.BlockSpec(memory_space=pltpu.SMEM), vmem, vmem, vmem),
+        scratch_shapes=[dma, dma],
+    )(update, momentum_new, load_block, norm_grads, norm_params, adam_m, adam_v)
+    return (update, momentum_new, owner_load, norm_params_new, adam_m_new, adam_v_new)
 
 
 def solution(mesh):

time: 62.4 us -> 60.8 us (0.974)
  local copies, waits for them, and re-layouts: 4.74 us -> 0 us
  Pallas kernels: 56 us -> 59.9 us
    pallas_call x0 -> x1, Pallas kernels: none -> 3.93 us  [on_device(): pl.pallas_call(finish, out_shape=(jax.ShapeDtypeStruct(update.shape, BF16...]
    unnamed x12 -> x0, local copies, waits for them, and re-layouts: 3.42 us -> none
    slice x1 -> x0, local copies, waits for them, and re-layouts: 1.33 us -> none  [on_device(): load_block[0, 0:1]]
    sub x1 -> x0, other arithmetic: 0.62 us -> none  [on_device(): norm_params_new = norm_params - adam_rate * corrected]
where the time goes in v3:
time: 60.8 us; the launch traced here: 60.6 us
  Pallas kernels  59.9 us (99%)
  between operations  0.64 us (1%)
    pallas_call x1, Pallas kernels, on_device(): pl.pallas_call(functools.partial(kernel, groups, parts, mats, 4), out_sha...  56 us
    pallas_call x1, Pallas kernels, on_device(): pl.pallas_call(finish, out_shape=(jax.ShapeDtypeStruct(update.shape, BF16...  3.93 us

profile of v3, /device:TPU:0, one launch (start us, length us, event | category | flops | bytes accessed | tf_op | source)
XLA Modules:
  0.0 60.6 jit_solution(9261226785505656631)
XLA Ops:
  0.6 56.0 %shard_map.118 = (bf16[14,32,1024]{2,1,0:T(8,128)(2,1)}, f32[14,32,1024]{2,1,0:T(8,128)}, f32[8,128]{1,0:T(8,128)}) custom-call(s32[14]{0:T(128)} %owners_hbm.1, bf16[14,32,1024]{2,1,0:T(8,128)(2,1)} %grads_hbm.1, f32[14,32,1024]{2,1,0:T(8,128)} %momentum_hbm.1), custom_call_target="tpu_custom_call" | custom-call | tf_op jit(solution)/shard_map/pallas_call | solution.py:333
  56.6 3.9 %shard_map.119 = (bf16[14,32,1024]{2,1,0:T(8,128)(2,1)}, f32[14,32,1024]{2,1,0:T(8,128)}, f32[1]{0:T(128)}, f32[14,128]{1,0:T(8,128)}, f32[14,128]{1,0:T(8,128)}, /*index=5*/f32[14,128]{1,0:T(8,128)}) custom-call(bf16[14,32,1024]{2,1,0:T(8,128)(2,1)} %get-tuple-element.9.update, f32[14,32,1024]{2,1,0:T(8,128)} %get-tuple-element.10.momentum, ...), custom_call_target="tpu_custom_call" | custom-call | tf_op jit(solution)/shard_map/pallas_call | solution.py:367
